TPU v7x, 32 devices: a whole 2x2x4 slice. The times are simulated.
32 devices in a mesh: mem: 8 (over y, x, core), lat: 4 (over z).
Axes of the slice: x: 2, y: 2, z: 4, core: 2. Of those that a mesh axis runs over, the one named last changes fastest.
Arguments:
- coarse_weights: bfloat16 [32, 32, 8, 128], P('lat', 'mem'), may hold values from -6 to 6
- perturbations: bfloat16 [32, 8, 128, 512], P('mem', None, 'lat'), may hold values from -6 to 6
- lat_matrix: bfloat16 [128, 32], P('lat'), may hold values from -1 to 1
- lon_matrix: bfloat16 [128, 512], replicated, may hold values from -0.5 to 0.5
- wind_field: float32 [2, 128, 512], P(None, 'lat', 'mem'), may hold values from -0.4 to 0.4
- observed_cell: int32 [4, 8, 128, 64], P(None, None, 'lat', 'mem'), may hold values from 0 to 7
- observed_value: float32 [4, 8, 128, 64], P(None, None, 'lat', 'mem'), may hold values from -6 to 6
- observed_weight: float32 [4, 8, 128, 64], P(None, None, 'lat', 'mem'), may hold values from 0.5 to 4
Outputs:
- gradient: float32 [32, 32, 8, 128], P('lat', 'mem')
- increment: float32 [8, 128, 512], P(None, 'lat', 'mem')
Inputs may be any that keep to these rules, and one draw needn't show every extreme that they name: `observed_cell`: the observed cell is an offset within its block of 8 longitudes.
All inputs are finite; a program needn't handle non-finite values.
Results may differ from a plain program's by a relative error of at most 0.0003.
Values may be sent and summed in bfloat16 or wider, within the bound.
A program may use at most 64 MiB of HBM per device.

v0:
```python
import jax
import jax.numpy as jnp
from jax import lax
from jax.sharding import PartitionSpec as P

STEPS = 4
OBLK = 8
diffusion = 0.2
highest = lax.Precision.HIGHEST


def padded_2(value, sides, width):
    for axis, dim in sides:
        peers, length = (lax.axis_size(axis), value.shape[dim])
        up = [(i, (i + 1) % peers) for i in range(peers - 1)]
        down = [(j, i) for i, j in up]
        last = lax.slice_in_dim(value, length - width, length, axis=dim)
        initial = lax.slice_in_dim(value, 0, width, axis=dim)
        before = lax.ppermute(last, axis, up)
        after = lax.ppermute(initial, axis, down)
        value = jnp.concatenate([before, value, after], axis=dim)
    return value


def stencil_parts(padded):
    center = padded[:, 1:-1, 1:-1]
    north_cell = padded[:, 2:, 1:-1]
    south_cell = padded[:, :-2, 1:-1]
    east_cell = padded[:, 1:-1, 2:]
    west_cell = padded[:, 1:-1, :-2]
    return (center, north_cell, south_cell, east_cell, west_cell)


def advance(padded, wind_out):
    center, north_cell, south_cell, east_cell, west_cell = stencil_parts(padded)
    spread = north_cell + south_cell + east_cell + west_cell - 4.0 * center
    return (
        center
        + diffusion * spread
        - 0.5 * wind_out[1] * (north_cell - south_cell)
        - 0.5 * wind_out[0] * (east_cell - west_cell)
    )


def retreat(padded, wind_in):
    center, north_cell, south_cell, east_cell, west_cell = stencil_parts(padded)
    spread = north_cell + south_cell + east_cell + west_cell - 4.0 * center
    along_lon = wind_in[0] * padded
    along_lat = wind_in[1] * padded
    return (
        center
        + diffusion * spread
        + 0.5 * (along_lat[:, 2:, 1:-1] - along_lat[:, :-2, 1:-1])
        + 0.5 * (along_lon[:, 1:-1, 2:] - along_lon[:, 1:-1, :-2])
    )


def observe(tangent, picked, observed, weighting):
    levels, row_count, col_count = tangent.shape
    blocks = tangent.reshape(levels, row_count, col_count // OBLK, OBLK)
    onehot = (picked[..., None] == jnp.arange(OBLK, dtype=jnp.int32)).astype(jnp.float32)
    looked = jnp.sum(blocks * onehot, axis=-1)
    misfit = weighting * (looked - observed)
    return (misfit[..., None] * onehot).reshape(levels, row_count, col_count)


def domain_mask(margin, row_count, col_count):
    lat_start = lax.axis_index("lat") * row_count - margin
    lon_start = lax.axis_index("mem") * col_count - margin
    row_place = lat_start + jnp.arange(row_count + 2 * margin, dtype=jnp.int32)
    col_place = lon_start + jnp.arange(col_count + 2 * margin, dtype=jnp.int32)
    rows_inside = (row_place >= 0) & (row_place < row_count * lax.axis_size("lat"))
    cols_inside = (col_place >= 0) & (col_place < col_count * lax.axis_size("mem"))
    return (rows_inside[:, None] & cols_inside[None, :]).astype(jnp.float32)


def body(
    coarse_weights,
    perturbations,
    lat_matrix,
    lon_matrix,
    wind_field,
    observed_cell,
    observed_value,
    observed_weight,
):
    members_here, levels, row_count, lon_total = perturbations.shape
    col_count = wind_field.shape[2]
    members_all = members_here * lax.axis_size("mem")
    member_scale = 1.0 / jnp.sqrt(jnp.float32(members_all - 1))
    lat_full = lat_matrix.astype(jnp.float32)
    lon_full = lon_matrix.astype(jnp.float32)
    widened = jnp.einsum(
        "cmlw,wf->cmlf", coarse_weights.astype(jnp.float32), lon_full, precision=highest
    )
    columns = lat_full
    localized = jnp.einsum(
        "rc,cmlf->mlrf",
        columns,
        lax.all_gather(widened, "lat", axis=0, tiled=True),
        precision=highest,
    )
    partial_sum = jnp.sum(localized * perturbations, axis=0)
    increment = lax.psum_scatter(partial_sum, "mem", scatter_dimension=2, tiled=True) * member_scale
    wide_wind = padded_2(wind_field, (("mem", 2), ("lat", 1)), STEPS)

    def wind_margin(margin):
        return wide_wind[
            :,
            STEPS - margin : STEPS + row_count + margin,
            STEPS - margin : STEPS + col_count + margin,
        ]

    forcings = []
    tangent = padded_2(increment, (("mem", 2), ("lat", 1)), STEPS)
    for step_index in range(STEPS):
        margin = STEPS - step_index - 1
        tangent = advance(tangent, wind_margin(margin)) * domain_mask(margin, row_count, col_count)
        inner = tangent[:, margin : margin + row_count, margin : margin + col_count]
        forcings.append(
            observe(
                inner,
                observed_cell[step_index],
                observed_value[step_index],
                observed_weight[step_index],
            )
        )
    adjoint = jnp.zeros_like(increment)
    for step_index in reversed(range(STEPS)):
        padded = padded_2(adjoint + forcings[step_index], (("mem", 2), ("lat", 1)), 1)
        adjoint = retreat(padded, wind_margin(1))
    product = perturbations * lax.all_gather(adjoint, "mem", axis=2, tiled=True)[None]
    projected = jnp.einsum("mlrf,wf->mlrw", product, lon_full, precision=highest)
    columns = lat_full
    banded = lax.psum_scatter(
        jnp.einsum("rc,mlrw->cmlw", columns, projected, precision=highest),
        "lat",
        scatter_dimension=0,
        tiled=True,
    )
    gradient = banded * member_scale + coarse_weights.astype(jnp.float32)
    return (gradient, increment)


def solution(mesh):
    in_specs = (
        P("lat", "mem", None, None),
        P("mem", None, "lat", None),
        P("lat", None),
        P(),
        P(None, "lat", "mem"),
        P(None, None, "lat", "mem"),
        P(None, None, "lat", "mem"),
        P(None, None, "lat", "mem"),
    )
    out_specs = (P("lat", "mem", None, None), P(None, "lat", "mem"))
    return jax.shard_map(body, mesh=mesh, in_specs=in_specs, out_specs=out_specs, check_vma=False)
```

profile of v0, /device:TPU:0, one launch (start us, length us, event | category | flops | bytes accessed | tf_op | source)
XLA Modules:
  0.0 257.9 jit_solution(16076721269377844049)
XLA Ops:
  8.1 1.9 fusion.53
  10.0 1.5 fusion.76
  11.5 2.4 collective-permute-start.4
  13.9 1.3 collective-permute-start.5
  19.0 39.5 %all-gather.2.cloned.1.call-done = f32[32,4,8,512]{3,0,2,1:T(8,128)} async-done(((f32[8,4,8,512]{3,0,2,1:T(8,128)}), f32[32,4,8,512]{3,0,2,1:T(8,128)}) %all-gather.2.cloned.1.call-update) | async-done | bytes 2097168 | tf_op jit(solution)/shard_map/all_gather | solution.py:100
  58.5 3.7 %fusion = f32[8,32,512]{2,1,0:T(8,128)} fusion(bf16[4,8,32,512]{3,2,1,0:T(8,128)(2,1)S(1)} %copy-done.1, f32[32,4,8,512]{3,0,2,1:T(8,128)} %all-gather.2.cloned.1.call-done, bf16[32,32]{1,0:T(8,128)(2,1)} %param.10), kind=kOutput, calls=%fused_computation.2 | convolution fusion | flops 202768384 | bytes 3672064 | tf_op jit(solution)/shard_map/rc,cmlf->mlrf/dot_general | solution.py:97
  62.2 1.8 copy.254
  64.1 1.4 reshape.260
  65.7 2.1 collective-permute-start.6
  67.8 1.3 collective-permute-start.7
  69.4 3.9 %collective-permute-done.7 = f32[2,4,72]{2,1,0:T(4,128)S(1)} collective-permute-done((f32[2,4,72]{2,1,0:T(4,128)S(1)}, f32[2,4,72]{2,1,0:T(4,128)S(1)}, u32[]{:S(2)}, u32[]{:S(2)}) %collective-permute-start.7) | collective-permute-done | bytes 2336 | tf_op jit(solution)/shard_map/ppermute | solution.py:20
  74.2 24.3 %reduce-scatter.7.cloned.1.call-done = f32[64,256]{1,0:T(8,128)} async-done(((f32[512,256]{1,0:T(8,128)}), f32[64,256]{1,0:T(8,128)}) %reduce-scatter.7.cloned.1.call-update) | async-done | bytes 65552
  99.8 1.3 collective-permute-start
  101.1 1.3 collective-permute-start.1
  102.5 3.5 %collective-permute-done.1 = f32[8,32,4]{2,1,0:T(8,128)S(1)} collective-permute-done((f32[8,32,4]{2,1,0:T(8,128)S(1)}, f32[8,32,4]{2,1,0:T(8,128)S(1)}, u32[]{:S(2)}, u32[]{:S(2)}) %collective-permute-start.1) | collective-permute-done | bytes 4128 | tf_op jit(solution)/shard_map/ppermute | solution.py:20
  106.3 3.4 %collective-permute-start.2 = (f32[8,4,72]{1,2,0:T(8,128)S(1)}, f32[8,4,72]{1,2,0:T(8,128)S(1)}, u32[]{:S(2)}, u32[]{:S(2)}) collective-permute-start(f32[8,4,72]{1,2,0:T(8,128)S(1)} %copy.233), channel_id=1, source_target_pairs={{0,1},{1,2},{2,3},{4,5},{5,6},{6,7},{8,9},{9,10},{10,11},{12,13},{... | collective-permute-start | bytes 27656 | tf_op jit(solution)/shard_map/ppermute | solution.py:19
  109.9 1.3 collective-permute-start.3
  112.1 2.5 collective-permute-done.2
  114.6 4.9 %collective-permute-done.3 = f32[8,4,72]{1,2,0:T(8,128)S(1)} collective-permute-done((f32[8,4,72]{1,2,0:T(8,128)S(1)}, f32[8,4,72]{1,2,0:T(8,128)S(1)}, u32[]{:S(2)}, u32[]{:S(2)}) %collective-permute-start.3) | collective-permute-done | bytes 9248 | tf_op jit(solution)/shard_map/ppermute | solution.py:20
  121.7 4.0 %collective-permute-start.8 = (f32[8,32,1]{1,2,0:T(1,128)S(1)}, f32[8,32,1]{1,2,0:T(1,128)S(1)}, u32[]{:S(2)}, u32[]{:S(2)}) collective-permute-start(f32[8,32,1]{1,2,0:T(1,128)S(1)} %get-tuple-element.40), channel_id=1, source_target_pairs={{0,4},{4,8},{8,12},{12,16},{16,20},{20,24},{24,28},{1,5},{5,9},{9,... | collective-permute-start | bytes 3080 | tf_op jit(solution)/shard_map/ppermute | solution.py:19
  125.8 1.3 collective-permute-start.9
  127.1 3.5 %collective-permute-done.9 = f32[8,32,1]{1,2,0:T(1,128)S(1)} collective-permute-done((f32[8,32,1]{1,2,0:T(1,128)S(1)}, f32[8,32,1]{1,2,0:T(1,128)S(1)}, u32[]{:S(2)}, u32[]{:S(2)}) %collective-permute-start.9) | collective-permute-done | bytes 1056 | tf_op jit(solution)/shard_map/ppermute | solution.py:20
  130.8 1.3 collective-permute-start.10
  132.1 4.6 %collective-permute-start.11 = (f32[8,1,66]{1,2,0:T(8,128)S(1)}, f32[8,1,66]{1,2,0:T(8,128)S(1)}, u32[]{:S(2)}, u32[]{:S(2)}) collective-permute-start(f32[8,1,66]{1,2,0:T(8,128)S(1)} %get-tuple-element.28), channel_id=1, source_target_pairs={{0,1},{1,2},{2,3},{4,5},{5,6},{6,7},{8,9},{9,10},{10,11},{12,13},{... | collective-permute-start | bytes 6344 | tf_op jit(solution)/shard_map/ppermute | solution.py:19
  136.8 4.3 %collective-permute-done.10 = f32[8,1,66]{1,2,0:T(8,128)S(1)} collective-permute-done((f32[8,1,66]{1,2,0:T(8,128)S(1)}, f32[8,1,66]{1,2,0:T(8,128)S(1)}, u32[]{:S(2)}, u32[]{:S(2)}) %collective-permute-start.10) | collective-permute-done | bytes 2144 | tf_op jit(solution)/shard_map/ppermute | solution.py:20
  141.1 1.7 collective-permute-done.11
  143.7 3.1 %collective-permute-start.12 = (f32[8,32,1]{1,2,0:T(1,128)S(1)}, f32[8,32,1]{1,2,0:T(1,128)S(1)}, u32[]{:S(2)}, u32[]{:S(2)}) collective-permute-start(f32[8,32,1]{1,2,0:T(1,128)S(1)} %get-tuple-element.38), channel_id=1, source_target_pairs={{0,4},{4,8},{8,12},{12,16},{16,20},{20,24},{24,28},{1,5},{5,9},{9,... | collective-permute-start | bytes 3080 | tf_op jit(solution)/shard_map/ppermute | solution.py:19
  148.1 1.8 collective-permute-done.13
  150.1 1.3 collective-permute-start.14
  151.4 4.9 %collective-permute-start.15 = (f32[8,1,66]{1,2,0:T(8,128)S(1)}, f32[8,1,66]{1,2,0:T(8,128)S(1)}, u32[]{:S(2)}, u32[]{:S(2)}) collective-permute-start(f32[8,1,66]{1,2,0:T(8,128)S(1)} %get-tuple-element.26), channel_id=1, source_target_pairs={{0,1},{1,2},{2,3},{4,5},{5,6},{6,7},{8,9},{9,10},{10,11},{12,13},{... | collective-permute-start | bytes 6344 | tf_op jit(solution)/shard_map/ppermute | solution.py:19
  156.3 4.1 %collective-permute-done.14 = f32[8,1,66]{1,2,0:T(8,128)S(1)} collective-permute-done((f32[8,1,66]{1,2,0:T(8,128)S(1)}, f32[8,1,66]{1,2,0:T(8,128)S(1)}, u32[]{:S(2)}, u32[]{:S(2)}) %collective-permute-start.14) | collective-permute-done | bytes 2144 | tf_op jit(solution)/shard_map/ppermute | solution.py:20
  160.4 1.7 collective-permute-done.15
  162.9 3.5 %collective-permute-start.16 = (f32[8,32,1]{1,2,0:T(1,128)S(1)}, f32[8,32,1]{1,2,0:T(1,128)S(1)}, u32[]{:S(2)}, u32[]{:S(2)}) collective-permute-start(f32[8,32,1]{1,2,0:T(1,128)S(1)} %get-tuple-element.36), channel_id=1, source_target_pairs={{0,4},{4,8},{8,12},{12,16},{16,20},{20,24},{24,28},{1,5},{5,9},{9,... | collective-permute-start | bytes 3080 | tf_op jit(solution)/shard_map/ppermute | solution.py:19
  167.8 1.8 collective-permute-done.17
  169.7 1.3 collective-permute-start.18
  171.0 5.0 %collective-permute-start.19 = (f32[8,1,66]{1,2,0:T(8,128)S(1)}, f32[8,1,66]{1,2,0:T(8,128)S(1)}, u32[]{:S(2)}, u32[]{:S(2)}) collective-permute-start(f32[8,1,66]{1,2,0:T(8,128)S(1)} %get-tuple-element.24), channel_id=1, source_target_pairs={{0,1},{1,2},{2,3},{4,5},{5,6},{6,7},{8,9},{9,10},{10,11},{12,13},{... | collective-permute-start | bytes 6344 | tf_op jit(solution)/shard_map/ppermute | solution.py:19
  176.0 4.2 %collective-permute-done.18 = f32[8,1,66]{1,2,0:T(8,128)S(1)} collective-permute-done((f32[8,1,66]{1,2,0:T(8,128)S(1)}, f32[8,1,66]{1,2,0:T(8,128)S(1)}, u32[]{:S(2)}, u32[]{:S(2)}) %collective-permute-start.18) | collective-permute-done | bytes 2144 | tf_op jit(solution)/shard_map/ppermute | solution.py:20
  180.2 1.7 collective-permute-done.19
  182.7 3.5 %collective-permute-start.20 = (f32[8,32,1]{1,2,0:T(1,128)S(1)}, f32[8,32,1]{1,2,0:T(1,128)S(1)}, u32[]{:S(2)}, u32[]{:S(2)}) collective-permute-start(f32[8,32,1]{1,2,0:T(1,128)S(1)} %get-tuple-element.30), channel_id=1, source_target_pairs={{0,4},{4,8},{8,12},{12,16},{16,20},{20,24},{24,28},{1,5},{5,9},{9,... | collective-permute-start | bytes 3080 | tf_op jit(solution)/shard_map/ppermute | solution.py:19
  186.2 1.3 collective-permute-start.21
  187.5 2.0 collective-permute-done.21
  190.9 5.0 %collective-permute-start.23 = (f32[8,1,66]{1,2,0:T(8,128)S(1)}, f32[8,1,66]{1,2,0:T(8,128)S(1)}, u32[]{:S(2)}, u32[]{:S(2)}) collective-permute-start(f32[8,1,66]{1,2,0:T(8,128)S(1)} %get-tuple-element.22), channel_id=1, source_target_pairs={{0,1},{1,2},{2,3},{4,5},{5,6},{6,7},{8,9},{9,10},{10,11},{12,13},{... | collective-permute-start | bytes 6344 | tf_op jit(solution)/shard_map/ppermute | solution.py:19
  196.0 4.2 %collective-permute-done.22 = f32[8,1,66]{1,2,0:T(8,128)S(1)} collective-permute-done((f32[8,1,66]{1,2,0:T(8,128)S(1)}, f32[8,1,66]{1,2,0:T(8,128)S(1)}, u32[]{:S(2)}, u32[]{:S(2)}) %collective-permute-start.22) | collective-permute-done | bytes 2144 | tf_op jit(solution)/shard_map/ppermute | solution.py:20
  200.2 1.7 collective-permute-done.23
  202.7 17.4 %all_gather.7 = f32[8,32,512]{1,2,0:T(8,128)S(1)} all-gather(f32[8,32,64]{1,2,0:T(8,128)S(1)} %fusion.4), channel_id=1, replica_groups=mesh['mem'=8,'lat'=4] {'mem'}, dimensions={2}, use_global_device_ids=true | all-gather | bytes 589824 | tf_op jit(solution)/shard_map/all_gather | solution.py:132
  220.1 1.4 copy.246
  221.5 2.2 fusion.1
  225.0 24.8 %reduce-scatter.5.cloned.1.call-done = f32[8,4,8,128]{3,0,2,1:T(8,128)} async-done(((f32[32,4,8,128]{3,0,2,1:T(8,128)}), f32[8,4,8,128]{3,0,2,1:T(8,128)}) %reduce-scatter.5.cloned.1.call-update) | async-done | bytes 131088 | tf_op jit(solution)/shard_map/reduce_scatter | solution.py:135
  (114 shorter events, 21.6 us)
Async XLA Ops:
  7.2 0.9 copy-start
  7.2 51.3 %copy-start.1 = (bf16[4,8,32,512]{3,2,1,0:T(8,128)(2,1)S(1)}, bf16[4,8,32,512]{3,2,1,0:T(8,128)(2,1)}, u32[]{:S(2)}) copy-start(bf16[4,8,32,512]{3,2,1,0:T(8,128)(2,1)} %param.9) | copy-start | bytes 3145732
  7.2 51.3 %all-gather.2.cloned.1.call-start = ((), (), s32[]{:S(2)}) async-start(), calls=%async_computation.2 | async-start | bytes 2621440 | tf_op jit(solution)/shard_map/all_gather | solution.py:100
  10.0 88.6 %reduce-scatter.7.cloned.1.call-start = ((), (), s32[]{:S(2)}) async-start(), calls=%async_computation.4 | async-start | bytes 589824
  11.5 54.0 %collective-permute-start.4 = (f32[2,32,4]{2,1,0:T(8,128)}, f32[2,32,4]{2,1,0:T(8,128)S(1)}, u32[]{:S(2)}, u32[]{:S(2)}) collective-permute-start(f32[2,32,4]{2,1,0:T(8,128)} %get-tuple-element.62), channel_id=1, source_target_pairs={{0,4},{4,8},{8,12},{12,16},{16,20},{20,24},{24,28},{1,5},{5,9},{9,... | collective-permute-start | bytes 3080 | tf_op jit(solution)/shard_map/ppermute | solution.py:19
  13.9 51.6 %collective-permute-start.5 = (f32[2,32,4]{2,1,0:T(8,128)}, f32[2,32,4]{2,1,0:T(8,128)S(1)}, u32[]{:S(2)}, u32[]{:S(2)}) collective-permute-start(f32[2,32,4]{2,1,0:T(8,128)} %get-tuple-element.63), channel_id=1, source_target_pairs={{4,0},{8,4},{12,8},{16,12},{20,16},{24,20},{28,24},{5,1},{9,5},{13... | collective-permute-start | bytes 3080 | tf_op jit(solution)/shard_map/ppermute | solution.py:20
  64.1 1.5 copy-start.3
  65.5 184.3 %reduce-scatter.5.cloned.1.call-start = ((), (), s32[]{:S(2)}) async-start(), calls=%async_computation.3 | async-start | bytes 655360 | tf_op jit(solution)/shard_map/reduce_scatter | solution.py:135
  65.6 2.2 copy-start.8
  65.6 3.6 %copy-start.9 = (f32[2,32,4]{2,1,0:T(8,128)}, f32[2,32,4]{2,1,0:T(8,128)S(1)}, u32[]{:S(2)}) copy-start(f32[2,32,4]{2,1,0:T(8,128)S(1)} %collective-permute-done.5) | copy-start | bytes 3076
  65.7 3.7 %collective-permute-start.6 = (f32[2,4,72]{2,1,0:T(4,128)S(1)}, f32[2,4,72]{2,1,0:T(4,128)S(1)}, u32[]{:S(2)}, u32[]{:S(2)}) collective-permute-start(f32[2,4,72]{2,1,0:T(4,128)S(1)} %get-tuple-element.50), channel_id=1, source_target_pairs={{0,1},{1,2},{2,3},{4,5},{5,6},{6,7},{8,9},{9,10},{10,11},{12,13},{... | collective-permute-start | bytes 6920 | tf_op jit(solution)/shard_map/ppermute | solution.py:19
  67.8 5.5 %collective-permute-start.7 = (f32[2,4,72]{2,1,0:T(4,128)S(1)}, f32[2,4,72]{2,1,0:T(4,128)S(1)}, u32[]{:S(2)}, u32[]{:S(2)}) collective-permute-start(f32[2,4,72]{2,1,0:T(4,128)S(1)} %get-tuple-element.51), channel_id=1, source_target_pairs={{1,0},{2,1},{3,2},{5,4},{6,5},{7,6},{9,8},{10,9},{11,10},{13,12},{... | collective-permute-start | bytes 6920 | tf_op jit(solution)/shard_map/ppermute | solution.py:20
  99.6 20.0 %copy-start.7 = (f32[38,70]{0,1:T(8,128)S(1)}, f32[38,70]{0,1:T(8,128)}, u32[]{:S(2)}) copy-start(f32[38,70]{0,1:T(8,128)} %and_convert_fusion.2) | copy-start | bytes 31924
  99.7 20.4 %copy-start.2 = (f32[8,32,64]{2,1,0:T(8,128)}, f32[8,32,64]{2,1,0:T(8,128)S(1)}, u32[]{:S(2)}) copy-start(f32[8,32,64]{2,1,0:T(8,128)S(1)} %broadcast_multiply_fusion.8) | copy-start | bytes 196612
  99.8 2.7 %collective-permute-start = (f32[8,32,4]{2,1,0:T(8,128)S(1)}, f32[8,32,4]{2,1,0:T(8,128)S(1)}, u32[]{:S(2)}, u32[]{:S(2)}) collective-permute-start(f32[8,32,4]{2,1,0:T(8,128)S(1)} %get-tuple-element.48), channel_id=1, source_target_pairs={{0,4},{4,8},{8,12},{12,16},{16,20},{20,24},{24,28},{1,5},{5,9},{9,... | collective-permute-start | bytes 12296 | tf_op jit(solution)/shard_map/ppermute | solution.py:19
  101.1 4.9 %collective-permute-start.1 = (f32[8,32,4]{2,1,0:T(8,128)S(1)}, f32[8,32,4]{2,1,0:T(8,128)S(1)}, u32[]{:S(2)}, u32[]{:S(2)}) collective-permute-start(f32[8,32,4]{2,1,0:T(8,128)S(1)} %get-tuple-element.49), channel_id=1, source_target_pairs={{4,0},{8,4},{12,8},{16,12},{20,16},{24,20},{28,24},{5,1},{9,5},{13... | collective-permute-start | bytes 12296 | tf_op jit(solution)/shard_map/ppermute | solution.py:20
  106.3 8.2 %collective-permute-start.2 = (f32[8,4,72]{1,2,0:T(8,128)S(1)}, f32[8,4,72]{1,2,0:T(8,128)S(1)}, u32[]{:S(2)}, u32[]{:S(2)}) collective-permute-start(f32[8,4,72]{1,2,0:T(8,128)S(1)} %copy.233), channel_id=1, source_target_pairs={{0,1},{1,2},{2,3},{4,5},{5,6},{6,7},{8,9},{9,10},{10,11},{12,13},{... | collective-permute-start | bytes 27656 | tf_op jit(solution)/shard_map/ppermute | solution.py:19
  109.8 10.3 %copy-start.6 = (f32[36,68]{0,1:T(8,128)S(1)}, f32[36,68]{0,1:T(8,128)}, u32[]{:S(2)}) copy-start(f32[36,68]{0,1:T(8,128)} %and_convert_fusion.1) | copy-start | bytes 29380
  109.9 9.5 %collective-permute-start.3 = (f32[8,4,72]{1,2,0:T(8,128)S(1)}, f32[8,4,72]{1,2,0:T(8,128)S(1)}, u32[]{:S(2)}, u32[]{:S(2)}) collective-permute-start(f32[8,4,72]{1,2,0:T(8,128)S(1)} %copy.234), channel_id=1, source_target_pairs={{1,0},{2,1},{3,2},{5,4},{6,5},{7,6},{9,8},{10,9},{11,10},{13,12},{... | collective-permute-start | bytes 27656 | tf_op jit(solution)/shard_map/ppermute | solution.py:20
  119.7 1.1 copy-start.5
  120.5 1.1 copy-start.10
  120.5 1.1 copy-start.11
  121.7 5.3 %collective-permute-start.8 = (f32[8,32,1]{1,2,0:T(1,128)S(1)}, f32[8,32,1]{1,2,0:T(1,128)S(1)}, u32[]{:S(2)}, u32[]{:S(2)}) collective-permute-start(f32[8,32,1]{1,2,0:T(1,128)S(1)} %get-tuple-element.40), channel_id=1, source_target_pairs={{0,4},{4,8},{8,12},{12,16},{16,20},{20,24},{24,28},{1,5},{5,9},{9,... | collective-permute-start | bytes 3080 | tf_op jit(solution)/shard_map/ppermute | solution.py:19
  125.8 4.8 %collective-permute-start.9 = (f32[8,32,1]{1,2,0:T(1,128)S(1)}, f32[8,32,1]{1,2,0:T(1,128)S(1)}, u32[]{:S(2)}, u32[]{:S(2)}) collective-permute-start(f32[8,32,1]{1,2,0:T(1,128)S(1)} %get-tuple-element.41), channel_id=1, source_target_pairs={{4,0},{8,4},{12,8},{16,12},{20,16},{24,20},{28,24},{5,1},{9,5},{13... | collective-permute-start | bytes 3080 | tf_op jit(solution)/shard_map/ppermute | solution.py:20
  130.8 10.4 %collective-permute-start.10 = (f32[8,1,66]{1,2,0:T(8,128)S(1)}, f32[8,1,66]{1,2,0:T(8,128)S(1)}, u32[]{:S(2)}, u32[]{:S(2)}) collective-permute-start(f32[8,1,66]{1,2,0:T(8,128)S(1)} %get-tuple-element.29), channel_id=1, source_target_pairs={{1,0},{2,1},{3,2},{5,4},{6,5},{7,6},{9,8},{10,9},{11,10},{13,12},{... | collective-permute-start | bytes 6344 | tf_op jit(solution)/shard_map/ppermute | solution.py:20
  132.1 10.8 %collective-permute-start.11 = (f32[8,1,66]{1,2,0:T(8,128)S(1)}, f32[8,1,66]{1,2,0:T(8,128)S(1)}, u32[]{:S(2)}, u32[]{:S(2)}) collective-permute-start(f32[8,1,66]{1,2,0:T(8,128)S(1)} %get-tuple-element.28), channel_id=1, source_target_pairs={{0,1},{1,2},{2,3},{4,5},{5,6},{6,7},{8,9},{9,10},{10,11},{12,13},{... | collective-permute-start | bytes 6344 | tf_op jit(solution)/shard_map/ppermute | solution.py:19
  143.7 4.5 %collective-permute-start.12 = (f32[8,32,1]{1,2,0:T(1,128)S(1)}, f32[8,32,1]{1,2,0:T(1,128)S(1)}, u32[]{:S(2)}, u32[]{:S(2)}) collective-permute-start(f32[8,32,1]{1,2,0:T(1,128)S(1)} %get-tuple-element.38), channel_id=1, source_target_pairs={{0,4},{4,8},{8,12},{12,16},{16,20},{20,24},{24,28},{1,5},{5,9},{9,... | collective-permute-start | bytes 3080 | tf_op jit(solution)/shard_map/ppermute | solution.py:19
  146.8 3.1 %collective-permute-start.13 = (f32[8,32,1]{1,2,0:T(1,128)S(1)}, f32[8,32,1]{1,2,0:T(1,128)S(1)}, u32[]{:S(2)}, u32[]{:S(2)}) collective-permute-start(f32[8,32,1]{1,2,0:T(1,128)S(1)} %get-tuple-element.39), channel_id=1, source_target_pairs={{4,0},{8,4},{12,8},{16,12},{20,16},{24,20},{28,24},{5,1},{9,5},{13... | collective-permute-start | bytes 3080 | tf_op jit(solution)/shard_map/ppermute | solution.py:20
  150.1 10.3 %collective-permute-start.14 = (f32[8,1,66]{1,2,0:T(8,128)S(1)}, f32[8,1,66]{1,2,0:T(8,128)S(1)}, u32[]{:S(2)}, u32[]{:S(2)}) collective-permute-start(f32[8,1,66]{1,2,0:T(8,128)S(1)} %get-tuple-element.27), channel_id=1, source_target_pairs={{1,0},{2,1},{3,2},{5,4},{6,5},{7,6},{9,8},{10,9},{11,10},{13,12},{... | collective-permute-start | bytes 6344 | tf_op jit(solution)/shard_map/ppermute | solution.py:20
  151.4 10.8 %collective-permute-start.15 = (f32[8,1,66]{1,2,0:T(8,128)S(1)}, f32[8,1,66]{1,2,0:T(8,128)S(1)}, u32[]{:S(2)}, u32[]{:S(2)}) collective-permute-start(f32[8,1,66]{1,2,0:T(8,128)S(1)} %get-tuple-element.26), channel_id=1, source_target_pairs={{0,1},{1,2},{2,3},{4,5},{5,6},{6,7},{8,9},{9,10},{10,11},{12,13},{... | collective-permute-start | bytes 6344 | tf_op jit(solution)/shard_map/ppermute | solution.py:19
  162.9 4.8 %collective-permute-start.16 = (f32[8,32,1]{1,2,0:T(1,128)S(1)}, f32[8,32,1]{1,2,0:T(1,128)S(1)}, u32[]{:S(2)}, u32[]{:S(2)}) collective-permute-start(f32[8,32,1]{1,2,0:T(1,128)S(1)} %get-tuple-element.36), channel_id=1, source_target_pairs={{0,4},{4,8},{8,12},{12,16},{16,20},{20,24},{24,28},{1,5},{5,9},{9,... | collective-permute-start | bytes 3080 | tf_op jit(solution)/shard_map/ppermute | solution.py:19
  166.5 3.1 %collective-permute-start.17 = (f32[8,32,1]{1,2,0:T(1,128)S(1)}, f32[8,32,1]{1,2,0:T(1,128)S(1)}, u32[]{:S(2)}, u32[]{:S(2)}) collective-permute-start(f32[8,32,1]{1,2,0:T(1,128)S(1)} %get-tuple-element.37), channel_id=1, source_target_pairs={{4,0},{8,4},{12,8},{16,12},{20,16},{24,20},{28,24},{5,1},{9,5},{13... | collective-permute-start | bytes 3080 | tf_op jit(solution)/shard_map/ppermute | solution.py:20
  169.7 10.4 %collective-permute-start.18 = (f32[8,1,66]{1,2,0:T(8,128)S(1)}, f32[8,1,66]{1,2,0:T(8,128)S(1)}, u32[]{:S(2)}, u32[]{:S(2)}) collective-permute-start(f32[8,1,66]{1,2,0:T(8,128)S(1)} %get-tuple-element.25), channel_id=1, source_target_pairs={{1,0},{2,1},{3,2},{5,4},{6,5},{7,6},{9,8},{10,9},{11,10},{13,12},{... | collective-permute-start | bytes 6344 | tf_op jit(solution)/shard_map/ppermute | solution.py:20
  171.0 10.9 %collective-permute-start.19 = (f32[8,1,66]{1,2,0:T(8,128)S(1)}, f32[8,1,66]{1,2,0:T(8,128)S(1)}, u32[]{:S(2)}, u32[]{:S(2)}) collective-permute-start(f32[8,1,66]{1,2,0:T(8,128)S(1)} %get-tuple-element.24), channel_id=1, source_target_pairs={{0,1},{1,2},{2,3},{4,5},{5,6},{6,7},{8,9},{9,10},{10,11},{12,13},{... | collective-permute-start | bytes 6344 | tf_op jit(solution)/shard_map/ppermute | solution.py:19
  182.7 4.8 %collective-permute-start.20 = (f32[8,32,1]{1,2,0:T(1,128)S(1)}, f32[8,32,1]{1,2,0:T(1,128)S(1)}, u32[]{:S(2)}, u32[]{:S(2)}) collective-permute-start(f32[8,32,1]{1,2,0:T(1,128)S(1)} %get-tuple-element.30), channel_id=1, source_target_pairs={{0,4},{4,8},{8,12},{12,16},{16,20},{20,24},{24,28},{1,5},{5,9},{9,... | collective-permute-start | bytes 3080 | tf_op jit(solution)/shard_map/ppermute | solution.py:19
  186.2 3.3 %collective-permute-start.21 = (f32[8,32,1]{1,2,0:T(1,128)S(1)}, f32[8,32,1]{1,2,0:T(1,128)S(1)}, u32[]{:S(2)}, u32[]{:S(2)}) collective-permute-start(f32[8,32,1]{1,2,0:T(1,128)S(1)} %get-tuple-element.31), channel_id=1, source_target_pairs={{4,0},{8,4},{12,8},{16,12},{20,16},{24,20},{28,24},{5,1},{9,5},{13... | collective-permute-start | bytes 3080 | tf_op jit(solution)/shard_map/ppermute | solution.py:20
  189.6 10.6 %collective-permute-start.22 = (f32[8,1,66]{1,2,0:T(8,128)S(1)}, f32[8,1,66]{1,2,0:T(8,128)S(1)}, u32[]{:S(2)}, u32[]{:S(2)}) collective-permute-start(f32[8,1,66]{1,2,0:T(8,128)S(1)} %get-tuple-element.23), channel_id=1, source_target_pairs={{1,0},{2,1},{3,2},{5,4},{6,5},{7,6},{9,8},{10,9},{11,10},{13,12},{... | collective-permute-start | bytes 6344 | tf_op jit(solution)/shard_map/ppermute | solution.py:20
  190.9 11.0 %collective-permute-start.23 = (f32[8,1,66]{1,2,0:T(8,128)S(1)}, f32[8,1,66]{1,2,0:T(8,128)S(1)}, u32[]{:S(2)}, u32[]{:S(2)}) collective-permute-start(f32[8,1,66]{1,2,0:T(8,128)S(1)} %get-tuple-element.22), channel_id=1, source_target_pairs={{0,1},{1,2},{2,3},{4,5},{5,6},{6,7},{8,9},{9,10},{10,11},{12,13},{... | collective-permute-start | bytes 6344 | tf_op jit(solution)/shard_map/ppermute | solution.py:19
  220.1 3.6 %copy-start.12 = (bf16[32,32]{1,0:T(8,128)(2,1)S(1)}, bf16[32,32]{1,0:T(8,128)(2,1)}, u32[]{:S(2)}) copy-start(bf16[32,32]{1,0:T(8,128)(2,1)} %param.10) | copy-start | bytes 6148
  221.5 28.3 %copy-start.4 = (bf16[8,4,8,128]{3,2,1,0:T(8,128)(2,1)S(1)}, bf16[8,4,8,128]{3,2,1,0:T(8,128)(2,1)}, u32[]{:S(2)}) copy-start(bf16[8,4,8,128]{3,2,1,0:T(8,128)(2,1)} %param.8) | copy-start | bytes 196612
Sparse Core Ops, SparseCore 0:
  10.1 48.3 all-gather.1
  65.6 32.8 reduce-scatter.6
  225.1 24.6 reduce-scatter.4
where the time goes:
time: 259 us; the launch traced here: 258 us
  waiting for transfers between devices  136 us (53%)
  starting transfers between devices  58.4 us (23%)
  blocking collectives  17.4 us (7%)
  between operations  14.5 us (6%)
  local copies, waits for them, and re-layouts  11.8 us (5%)
  other arithmetic  10.6 us (4%)
  matrix products  9.04 us (3%)
    ppermute x12, starting transfers between devices, padded_2(): before = lax.ppermute(last, axis, up)  42.8 us
    all_gather x1, waiting for transfers between devices, body(): lax.all_gather(widened, 'lat', axis=0, tiled=True)  39.5 us
    ppermute x12, waiting for transfers between devices, padded_2(): after = lax.ppermute(initial, axis, down)  38.1 us
    reduce_scatter x1, waiting for transfers between devices, body(): lax.psum_scatter(jnp.einsum('rc,mlrw->cmlw', columns, projected, precisio...  24.8 us
    unnamed x4, waiting for transfers between devices  24.4 us
    all_gather x1, blocking collectives, body(): lax.all_gather(adjoint, 'mem', axis=2, tiled=True)[None]  17.4 us
    ppermute x12, starting transfers between devices, padded_2(): after = lax.ppermute(initial, axis, down)  15.5 us
    ppermute x12, waiting for transfers between devices, padded_2(): before = lax.ppermute(last, axis, up)  9.46 us
  transfers between devices with their start and end apart: 27, of which 19 were waited for; matrix products, arithmetic and copies ran while one was open for 6% of the time, Pallas kernels for 0%

commit v1 on v0

--- a/solution.py
+++ b/solution.py
@@ -7,6 +7,25 @@
 OBLK = 8
 diffusion = 0.2
 highest = lax.Precision.HIGHEST
+
+
+def gather_around(shard, axis, dim):
+    size, here, rows = (lax.axis_size(axis), lax.axis_index(axis), shard.shape[dim])
+    right = [(i, (i + 1) % size) for i in range(size)]
+    behind = [(i, (i - 1) % size) for i in range(size)]
+    out = jnp.zeros((*shard.shape[:dim], size * rows, *shard.shape[dim + 1 :]), shard.dtype)
+    out = lax.dynamic_update_slice_in_dim(out, shard, here * rows, axis=dim)
+    from_left = from_right = shard
+    half = size // 2
+    for turn in range(1, half + 1):
+        from_left = lax.ppermute(from_left, axis, right)
+        out = lax.dynamic_update_slice_in_dim(out, from_left, (here - turn) % size * rows, axis=dim)
+        if turn < size - half:
+            from_right = lax.ppermute(from_right, axis, behind)
+            out = lax.dynamic_update_slice_in_dim(
+                out, from_right, (here + turn) % size * rows, axis=dim
+            )
+    return out
 
 
 def padded_2(value, sides, width):
@@ -129,7 +148,7 @@
     for step_index in reversed(range(STEPS)):
         padded = padded_2(adjoint + forcings[step_index], (("mem", 2), ("lat", 1)), 1)
         adjoint = retreat(padded, wind_margin(1))
-    product = perturbations * lax.all_gather(adjoint, "mem", axis=2, tiled=True)[None]
+    product = perturbations * gather_around(adjoint, "mem", 2)[None]
     projected = jnp.einsum("mlrf,wf->mlrw", product, lon_full, precision=highest)
     columns = lat_full
     banded = lax.psum_scatter(

time: 259 us -> 274 us (1.058)
  blocking collectives: 17.4 us -> 0 us
  waiting for transfers between devices: 136 us -> 149 us
  starting transfers between devices: 58.4 us -> 69 us
  local copies, waits for them, and re-layouts: 11.8 us -> 21.6 us
    all_gather x1 -> x0, blocking collectives: 17.4 us -> none  [body(): lax.all_gather(adjoint, 'mem', axis=2, tiled=True)[None]]
    ppermute x0 -> x7, waiting for transfers between devices: none -> 10.7 us  [the longest x4 8.2 us: gather_around(): from_left = lax.ppermute(from_left, axis, right)]
    ppermute x0 -> x7, starting transfers between devices: none -> 10 us  [the longest x3 6.74 us: gather_around(): from_right = lax.ppermute(from_right, axis, behind)]
    dynamic_update_slice x0 -> x8, local copies, waits for them, and re-layouts: none -> 7.76 us  [the longest x4 3.79 us: gather_around(): lax.dynamic_update_slice_in_dim(out, from_left, (here - turn) % size * ro...]
    reduce_scatter x1, waiting for transfers between devices: 24.8 us -> 28.9 us  [body(): lax.psum_scatter(jnp.einsum('rc,mlrw->cmlw', columns, projected, precisio...]
    unnamed x31 -> x25, local copies, waits for them, and re-layouts: 5.89 us -> 5.86 us
  transfers between devices with their start and end apart: 27 -> 34, of which waited for: 19 -> 24; matrix products, arithmetic and copies ran while one was open for 6% -> 9% of each run, Pallas kernels for 0% -> 0%
where the time goes in v1:
time: 274 us; the launch traced here: 273 us
  waiting for transfers between devices  149 us (54%)
  starting transfers between devices  69 us (25%)
  local copies, waits for them, and re-layouts  21.6 us (8%)
  between operations  14.5 us (5%)
  other arithmetic  10.7 us (4%)
  matrix products  7.93 us (3%)
    ppermute x12, starting transfers between devices, padded_2(): before = lax.ppermute(last, axis, up)  43.4 us
    all_gather x1, waiting for transfers between devices, body(): lax.all_gather(widened, 'lat', axis=0, tiled=True)  40.2 us
    ppermute x12, waiting for transfers between devices, padded_2(): after = lax.ppermute(initial, axis, down)  36.6 us
    reduce_scatter x1, waiting for transfers between devices, body(): lax.psum_scatter(jnp.einsum('rc,mlrw->cmlw', columns, projected, precisio...  28.9 us
    unnamed x4, waiting for transfers between devices  23.1 us
    ppermute x12, starting transfers between devices, padded_2(): after = lax.ppermute(initial, axis, down)  15.5 us
    ppermute x12, waiting for transfers between devices, padded_2(): before = lax.ppermute(last, axis, up)  9.47 us
    ppermute x4, waiting for transfers between devices, gather_around(): from_left = lax.ppermute(from_left, axis, right)  8.2 us
  transfers between devices with their start and end apart: 34, of which 24 were waited for; matrix products, arithmetic and copies ran while one was open for 9% of the time, Pallas kernels for 0%

profile of v1, /device:TPU:0, one launch (start us, length us, event | category | flops | bytes accessed | tf_op | source)
XLA Modules:
  0.0 272.7 jit_solution(11452026398968652341)
XLA Ops:
  8.1 1.8 fusion.53
  10.0 1.5 fusion.76
  11.5 3.0 %collective-permute-start.4 = (f32[2,32,4]{2,1,0:T(8,128)}, f32[2,32,4]{2,1,0:T(8,128)}, u32[]{:S(2)}, u32[]{:S(2)}) collective-permute-start(f32[2,32,4]{2,1,0:T(8,128)} %get-tuple-element.62), channel_id=1, source_target_pairs={{0,4},{4,8},{8,12},{12,16},{16,20},{20,24},{24,28},{1,5},{5,9},{9,... | collective-permute-start | bytes 3080 | tf_op jit(solution)/shard_map/ppermute | solution.py:38
  16.2 1.3 multiply_bitcast_fusion.3
  18.3 40.2 %all-gather.2.cloned.1.call-done = f32[32,4,8,512]{3,0,2,1:T(8,128)} async-done(((f32[8,4,8,512]{3,0,2,1:T(8,128)}), f32[32,4,8,512]{3,0,2,1:T(8,128)}) %all-gather.2.cloned.1.call-update) | async-done | bytes 2097168 | tf_op jit(solution)/shard_map/all_gather | solution.py:119
  58.5 3.7 %fusion = f32[8,32,512]{2,1,0:T(8,128)} fusion(bf16[4,8,32,512]{3,2,1,0:T(8,128)(2,1)S(1)} %copy-done.1, f32[32,4,8,512]{3,0,2,1:T(8,128)} %all-gather.2.cloned.1.call-done, bf16[32,32]{1,0:T(8,128)(2,1)} %param.10), kind=kOutput, calls=%fused_computation.2 | convolution fusion | flops 202768384 | bytes 3672064 | tf_op jit(solution)/shard_map/rc,cmlf->mlrf/dot_general | solution.py:116
  62.2 1.8 copy.282
  64.0 1.4 reshape.299
  66.4 2.1 collective-permute-start.6
  71.5 2.4 collective-permute-done.7
  75.5 23.0 %reduce-scatter.7.cloned.1.call-done = f32[64,256]{1,0:T(8,128)} async-done(((f32[512,256]{1,0:T(8,128)}), f32[64,256]{1,0:T(8,128)}) %reduce-scatter.7.cloned.1.call-update) | async-done | bytes 65552
  99.8 1.3 collective-permute-start
  102.5 3.6 %collective-permute-done.1 = f32[8,32,4]{2,1,0:T(8,128)S(1)} collective-permute-done((f32[8,32,4]{2,1,0:T(8,128)S(1)}, f32[8,32,4]{2,1,0:T(8,128)S(1)}, u32[]{:S(2)}, u32[]{:S(2)}) %collective-permute-start.1) | collective-permute-done | bytes 4128 | tf_op jit(solution)/shard_map/ppermute | solution.py:39
  106.3 3.4 %collective-permute-start.2 = (f32[8,4,72]{1,2,0:T(8,128)S(1)}, f32[8,4,72]{1,2,0:T(8,128)S(1)}, u32[]{:S(2)}, u32[]{:S(2)}) collective-permute-start(f32[8,4,72]{1,2,0:T(8,128)S(1)} %copy.254), channel_id=1, source_target_pairs={{0,1},{1,2},{2,3},{4,5},{5,6},{6,7},{8,9},{9,10},{10,11},{12,13},{... | collective-permute-start | bytes 27656 | tf_op jit(solution)/shard_map/ppermute | solution.py:38
  112.0 2.5 collective-permute-done.2
  114.5 4.9 %collective-permute-done.3 = f32[8,4,72]{1,2,0:T(8,128)S(1)} collective-permute-done((f32[8,4,72]{1,2,0:T(8,128)S(1)}, f32[8,4,72]{1,2,0:T(8,128)S(1)}, u32[]{:S(2)}, u32[]{:S(2)}) %collective-permute-start.3) | collective-permute-done | bytes 9248 | tf_op jit(solution)/shard_map/ppermute | solution.py:39
  121.7 4.0 %collective-permute-start.8 = (f32[8,32,1]{1,2,0:T(1,128)S(1)}, f32[8,32,1]{1,2,0:T(1,128)S(1)}, u32[]{:S(2)}, u32[]{:S(2)}) collective-permute-start(f32[8,32,1]{1,2,0:T(1,128)S(1)} %get-tuple-element.40), channel_id=1, source_target_pairs={{0,4},{4,8},{8,12},{12,16},{16,20},{20,24},{24,28},{1,5},{5,9},{9,... | collective-permute-start | bytes 3080 | tf_op jit(solution)/shard_map/ppermute | solution.py:38
  127.0 3.5 %collective-permute-done.9 = f32[8,32,1]{1,2,0:T(1,128)S(1)} collective-permute-done((f32[8,32,1]{1,2,0:T(1,128)S(1)}, f32[8,32,1]{1,2,0:T(1,128)S(1)}, u32[]{:S(2)}, u32[]{:S(2)}) %collective-permute-start.9) | collective-permute-done | bytes 1056 | tf_op jit(solution)/shard_map/ppermute | solution.py:39
  132.0 4.6 %collective-permute-start.11 = (f32[8,1,66]{1,2,0:T(8,128)S(1)}, f32[8,1,66]{1,2,0:T(8,128)S(1)}, u32[]{:S(2)}, u32[]{:S(2)}) collective-permute-start(f32[8,1,66]{1,2,0:T(8,128)S(1)} %get-tuple-element.28), channel_id=1, source_target_pairs={{0,1},{1,2},{2,3},{4,5},{5,6},{6,7},{8,9},{9,10},{10,11},{12,13},{... | collective-permute-start | bytes 6344 | tf_op jit(solution)/shard_map/ppermute | solution.py:38
  136.8 4.3 %collective-permute-done.10 = f32[8,1,66]{1,2,0:T(8,128)S(1)} collective-permute-done((f32[8,1,66]{1,2,0:T(8,128)S(1)}, f32[8,1,66]{1,2,0:T(8,128)S(1)}, u32[]{:S(2)}, u32[]{:S(2)}) %collective-permute-start.10) | collective-permute-done | bytes 2144 | tf_op jit(solution)/shard_map/ppermute | solution.py:39
  141.1 1.7 collective-permute-done.11
  143.6 3.1 %collective-permute-start.12 = (f32[8,32,1]{1,2,0:T(1,128)S(1)}, f32[8,32,1]{1,2,0:T(1,128)S(1)}, u32[]{:S(2)}, u32[]{:S(2)}) collective-permute-start(f32[8,32,1]{1,2,0:T(1,128)S(1)} %get-tuple-element.38), channel_id=1, source_target_pairs={{0,4},{4,8},{8,12},{12,16},{16,20},{20,24},{24,28},{1,5},{5,9},{9,... | collective-permute-start | bytes 3080 | tf_op jit(solution)/shard_map/ppermute | solution.py:38
  148.1 1.8 collective-permute-done.13
  151.3 4.9 %collective-permute-start.15 = (f32[8,1,66]{1,2,0:T(8,128)S(1)}, f32[8,1,66]{1,2,0:T(8,128)S(1)}, u32[]{:S(2)}, u32[]{:S(2)}) collective-permute-start(f32[8,1,66]{1,2,0:T(8,128)S(1)} %get-tuple-element.26), channel_id=1, source_target_pairs={{0,1},{1,2},{2,3},{4,5},{5,6},{6,7},{8,9},{9,10},{10,11},{12,13},{... | collective-permute-start | bytes 6344 | tf_op jit(solution)/shard_map/ppermute | solution.py:38
  156.2 4.1 %collective-permute-done.14 = f32[8,1,66]{1,2,0:T(8,128)S(1)} collective-permute-done((f32[8,1,66]{1,2,0:T(8,128)S(1)}, f32[8,1,66]{1,2,0:T(8,128)S(1)}, u32[]{:S(2)}, u32[]{:S(2)}) %collective-permute-start.14) | collective-permute-done | bytes 2144 | tf_op jit(solution)/shard_map/ppermute | solution.py:39
  160.3 1.7 collective-permute-done.15
  162.9 3.5 %collective-permute-start.16 = (f32[8,32,1]{1,2,0:T(1,128)S(1)}, f32[8,32,1]{1,2,0:T(1,128)S(1)}, u32[]{:S(2)}, u32[]{:S(2)}) collective-permute-start(f32[8,32,1]{1,2,0:T(1,128)S(1)} %get-tuple-element.36), channel_id=1, source_target_pairs={{0,4},{4,8},{8,12},{12,16},{16,20},{20,24},{24,28},{1,5},{5,9},{9,... | collective-permute-start | bytes 3080 | tf_op jit(solution)/shard_map/ppermute | solution.py:38
  167.7 1.8 collective-permute-done.17
  170.9 5.0 %collective-permute-start.19 = (f32[8,1,66]{1,2,0:T(8,128)S(1)}, f32[8,1,66]{1,2,0:T(8,128)S(1)}, u32[]{:S(2)}, u32[]{:S(2)}) collective-permute-start(f32[8,1,66]{1,2,0:T(8,128)S(1)} %get-tuple-element.24), channel_id=1, source_target_pairs={{0,1},{1,2},{2,3},{4,5},{5,6},{6,7},{8,9},{9,10},{10,11},{12,13},{... | collective-permute-start | bytes 6344 | tf_op jit(solution)/shard_map/ppermute | solution.py:38
  175.9 4.2 %collective-permute-done.18 = f32[8,1,66]{1,2,0:T(8,128)S(1)} collective-permute-done((f32[8,1,66]{1,2,0:T(8,128)S(1)}, f32[8,1,66]{1,2,0:T(8,128)S(1)}, u32[]{:S(2)}, u32[]{:S(2)}) %collective-permute-start.18) | collective-permute-done | bytes 2144 | tf_op jit(solution)/shard_map/ppermute | solution.py:39
  180.1 1.7 collective-permute-done.19
  182.6 3.5 %collective-permute-start.20 = (f32[8,32,1]{1,2,0:T(1,128)S(1)}, f32[8,32,1]{1,2,0:T(1,128)S(1)}, u32[]{:S(2)}, u32[]{:S(2)}) collective-permute-start(f32[8,32,1]{1,2,0:T(1,128)S(1)} %get-tuple-element.30), channel_id=1, source_target_pairs={{0,4},{4,8},{8,12},{12,16},{16,20},{20,24},{24,28},{1,5},{5,9},{9,... | collective-permute-start | bytes 3080 | tf_op jit(solution)/shard_map/ppermute | solution.py:38
  187.4 2.0 collective-permute-done.21
  190.9 5.0 %collective-permute-start.23 = (f32[8,1,66]{1,2,0:T(8,128)S(1)}, f32[8,1,66]{1,2,0:T(8,128)S(1)}, u32[]{:S(2)}, u32[]{:S(2)}) collective-permute-start(f32[8,1,66]{1,2,0:T(8,128)S(1)} %get-tuple-element.22), channel_id=1, source_target_pairs={{0,1},{1,2},{2,3},{4,5},{5,6},{6,7},{8,9},{9,10},{10,11},{12,13},{... | collective-permute-start | bytes 6344 | tf_op jit(solution)/shard_map/ppermute | solution.py:38
  195.9 4.2 %collective-permute-done.22 = f32[8,1,66]{1,2,0:T(8,128)S(1)} collective-permute-done((f32[8,1,66]{1,2,0:T(8,128)S(1)}, f32[8,1,66]{1,2,0:T(8,128)S(1)}, u32[]{:S(2)}, u32[]{:S(2)}) %collective-permute-start.22) | collective-permute-done | bytes 2144 | tf_op jit(solution)/shard_map/ppermute | solution.py:39
  200.1 1.7 collective-permute-done.23
  202.6 1.6 collective-permute-start.24
  205.3 4.0 %collective-permute-done.24 = f32[8,32,64]{1,2,0:T(8,128)S(1)} collective-permute-done((f32[8,32,64]{1,2,0:T(8,128)S(1)}, f32[8,32,64]{1,2,0:T(8,128)S(1)}, u32[]{:S(2)}, u32[]{:S(2)}) %collective-permute-start.24) | collective-permute-done | bytes 65568 | tf_op jit(solution)/shard_map/ppermute | solution.py:21
  211.1 2.8 %collective-permute-start.27 = (f32[8,32,64]{1,2,0:T(8,128)S(1)}, f32[8,32,64]{1,2,0:T(8,128)S(1)}, u32[]{:S(2)}, u32[]{:S(2)}) collective-permute-start(f32[8,32,64]{1,2,0:T(8,128)S(1)} %collective-permute-done.25), channel_id=1, source_target_pairs={{0,28},{4,0},{8,4},{12,8},{16,12},{20,16},{24,20},{28,24},{1,29},{... | collective-permute-start | bytes 196616 | tf_op jit(solution)/shard_map/ppermute | solution.py:24
  213.9 2.3 collective-permute-done.26
  217.0 1.7 collective-permute-done.27
  218.7 2.8 %collective-permute-start.29 = (f32[8,32,64]{1,2,0:T(8,128)S(1)}, f32[8,32,64]{1,2,0:T(8,128)}, u32[]{:S(2)}, u32[]{:S(2)}) collective-permute-start(f32[8,32,64]{1,2,0:T(8,128)S(1)} %collective-permute-done.27), channel_id=1, source_target_pairs={{0,28},{4,0},{8,4},{12,8},{16,12},{20,16},{24,20},{28,24},{1,29},{... | collective-permute-start | bytes 196616 | tf_op jit(solution)/shard_map/ppermute | solution.py:24
  221.6 1.8 collective-permute-done.28
  224.1 1.5 dynamic_update_slice.41
  225.7 1.6 dynamic_update_slice.42
  228.5 1.6 dynamic_update_slice.45
  231.1 1.6 dynamic_update_slice.46
  235.7 28.9 %reduce-scatter.5.cloned.1.call-done = f32[8,4,8,128]{3,0,2,1:T(8,128)} async-done(((f32[32,4,8,128]{3,0,2,1:T(8,128)}), f32[8,4,8,128]{3,0,2,1:T(8,128)}) %reduce-scatter.5.cloned.1.call-update) | async-done | bytes 131088 | tf_op jit(solution)/shard_map/reduce_scatter | solution.py:154
  (137 shorter events, 41.8 us)
Async XLA Ops:
  7.2 0.9 copy-start
  7.2 51.3 %copy-start.1 = (bf16[4,8,32,512]{3,2,1,0:T(8,128)(2,1)S(1)}, bf16[4,8,32,512]{3,2,1,0:T(8,128)(2,1)}, u32[]{:S(2)}) copy-start(bf16[4,8,32,512]{3,2,1,0:T(8,128)(2,1)} %param.9) | copy-start | bytes 3145732
  7.2 51.3 %all-gather.2.cloned.1.call-start = ((), (), s32[]{:S(2)}) async-start(), calls=%async_computation.2 | async-start | bytes 2621440 | tf_op jit(solution)/shard_map/all_gather | solution.py:119
  9.9 88.6 %reduce-scatter.7.cloned.1.call-start = ((), (), s32[]{:S(2)}) async-start(), calls=%async_computation.4 | async-start | bytes 589824
  11.5 54.0 %collective-permute-start.4 = (f32[2,32,4]{2,1,0:T(8,128)}, f32[2,32,4]{2,1,0:T(8,128)}, u32[]{:S(2)}, u32[]{:S(2)}) collective-permute-start(f32[2,32,4]{2,1,0:T(8,128)} %get-tuple-element.62), channel_id=1, source_target_pairs={{0,4},{4,8},{8,12},{12,16},{16,20},{20,24},{24,28},{1,5},{5,9},{9,... | collective-permute-start | bytes 3080 | tf_op jit(solution)/shard_map/ppermute | solution.py:38
  14.5 51.0 %collective-permute-start.5 = (f32[2,32,4]{2,1,0:T(8,128)}, f32[2,32,4]{2,1,0:T(8,128)}, u32[]{:S(2)}, u32[]{:S(2)}) collective-permute-start(f32[2,32,4]{2,1,0:T(8,128)} %get-tuple-element.63), channel_id=1, source_target_pairs={{4,0},{8,4},{12,8},{16,12},{20,16},{24,20},{28,24},{5,1},{9,5},{13... | collective-permute-start | bytes 3080 | tf_op jit(solution)/shard_map/ppermute | solution.py:39
  64.0 1.5 copy-start.3
  65.4 199.1 %reduce-scatter.5.cloned.1.call-start = ((), (), s32[]{:S(2)}) async-start(), calls=%async_computation.3 | async-start | bytes 655360 | tf_op jit(solution)/shard_map/reduce_scatter | solution.py:154
  66.4 5.1 %collective-permute-start.6 = (f32[2,4,72]{2,1,0:T(4,128)S(1)}, f32[2,4,72]{2,1,0:T(4,128)S(1)}, u32[]{:S(2)}, u32[]{:S(2)}) collective-permute-start(f32[2,4,72]{2,1,0:T(4,128)S(1)} %get-tuple-element.50), channel_id=1, source_target_pairs={{0,1},{1,2},{2,3},{4,5},{5,6},{6,7},{8,9},{9,10},{10,11},{12,13},{... | collective-permute-start | bytes 6920 | tf_op jit(solution)/shard_map/ppermute | solution.py:38
  68.4 5.5 %collective-permute-start.7 = (f32[2,4,72]{2,1,0:T(4,128)S(1)}, f32[2,4,72]{2,1,0:T(4,128)S(1)}, u32[]{:S(2)}, u32[]{:S(2)}) collective-permute-start(f32[2,4,72]{2,1,0:T(4,128)S(1)} %get-tuple-element.51), channel_id=1, source_target_pairs={{1,0},{2,1},{3,2},{5,4},{6,5},{7,6},{9,8},{10,9},{11,10},{13,12},{... | collective-permute-start | bytes 6920 | tf_op jit(solution)/shard_map/ppermute | solution.py:39
  99.7 20.4 %copy-start.2 = (f32[8,32,64]{2,1,0:T(8,128)}, f32[8,32,64]{2,1,0:T(8,128)S(1)}, u32[]{:S(2)}) copy-start(f32[8,32,64]{2,1,0:T(8,128)S(1)} %broadcast_multiply_fusion.8) | copy-start | bytes 196612
  99.8 2.7 collective-permute-start
  101.1 4.9 %collective-permute-start.1 = (f32[8,32,4]{2,1,0:T(8,128)S(1)}, f32[8,32,4]{2,1,0:T(8,128)S(1)}, u32[]{:S(2)}, u32[]{:S(2)}) collective-permute-start(f32[8,32,4]{2,1,0:T(8,128)S(1)} %get-tuple-element.49), channel_id=1, source_target_pairs={{4,0},{8,4},{12,8},{16,12},{20,16},{24,20},{28,24},{5,1},{9,5},{13... | collective-permute-start | bytes 12296 | tf_op jit(solution)/shard_map/ppermute | solution.py:39
  106.3 8.2 %collective-permute-start.2 = (f32[8,4,72]{1,2,0:T(8,128)S(1)}, f32[8,4,72]{1,2,0:T(8,128)S(1)}, u32[]{:S(2)}, u32[]{:S(2)}) collective-permute-start(f32[8,4,72]{1,2,0:T(8,128)S(1)} %copy.254), channel_id=1, source_target_pairs={{0,1},{1,2},{2,3},{4,5},{5,6},{6,7},{8,9},{9,10},{10,11},{12,13},{... | collective-permute-start | bytes 27656 | tf_op jit(solution)/shard_map/ppermute | solution.py:38
  109.9 9.5 %collective-permute-start.3 = (f32[8,4,72]{1,2,0:T(8,128)S(1)}, f32[8,4,72]{1,2,0:T(8,128)S(1)}, u32[]{:S(2)}, u32[]{:S(2)}) collective-permute-start(f32[8,4,72]{1,2,0:T(8,128)S(1)} %copy.255), channel_id=1, source_target_pairs={{1,0},{2,1},{3,2},{5,4},{6,5},{7,6},{9,8},{10,9},{11,10},{13,12},{... | collective-permute-start | bytes 27656 | tf_op jit(solution)/shard_map/ppermute | solution.py:39
  120.4 1.1 copy-start.5
  120.4 1.1 copy-start.6
  121.1 15.5 %copy-start.8 = (f32[34,66]{1,0:T(8,128)S(1)}, f32[34,66]{1,0:T(8,128)}, u32[]{:S(2)}) copy-start(f32[34,66]{1,0:T(8,128)} %get-tuple-element.52) | copy-start | bytes 26932
  121.1 15.6 %copy-start.7 = (f32[34,66]{1,0:T(8,128)S(1)}, f32[34,66]{1,0:T(8,128)}, u32[]{:S(2)}) copy-start(f32[34,66]{1,0:T(8,128)} %get-tuple-element.53) | copy-start | bytes 26932
  121.7 5.3 %collective-permute-start.8 = (f32[8,32,1]{1,2,0:T(1,128)S(1)}, f32[8,32,1]{1,2,0:T(1,128)S(1)}, u32[]{:S(2)}, u32[]{:S(2)}) collective-permute-start(f32[8,32,1]{1,2,0:T(1,128)S(1)} %get-tuple-element.40), channel_id=1, source_target_pairs={{0,4},{4,8},{8,12},{12,16},{16,20},{20,24},{24,28},{1,5},{5,9},{9,... | collective-permute-start | bytes 3080 | tf_op jit(solution)/shard_map/ppermute | solution.py:38
  125.7 4.8 %collective-permute-start.9 = (f32[8,32,1]{1,2,0:T(1,128)S(1)}, f32[8,32,1]{1,2,0:T(1,128)S(1)}, u32[]{:S(2)}, u32[]{:S(2)}) collective-permute-start(f32[8,32,1]{1,2,0:T(1,128)S(1)} %get-tuple-element.41), channel_id=1, source_target_pairs={{4,0},{8,4},{12,8},{16,12},{20,16},{24,20},{28,24},{5,1},{9,5},{13... | collective-permute-start | bytes 3080 | tf_op jit(solution)/shard_map/ppermute | solution.py:39
  130.7 10.4 %collective-permute-start.10 = (f32[8,1,66]{1,2,0:T(8,128)S(1)}, f32[8,1,66]{1,2,0:T(8,128)S(1)}, u32[]{:S(2)}, u32[]{:S(2)}) collective-permute-start(f32[8,1,66]{1,2,0:T(8,128)S(1)} %get-tuple-element.29), channel_id=1, source_target_pairs={{1,0},{2,1},{3,2},{5,4},{6,5},{7,6},{9,8},{10,9},{11,10},{13,12},{... | collective-permute-start | bytes 6344 | tf_op jit(solution)/shard_map/ppermute | solution.py:39
  132.0 10.8 %collective-permute-start.11 = (f32[8,1,66]{1,2,0:T(8,128)S(1)}, f32[8,1,66]{1,2,0:T(8,128)S(1)}, u32[]{:S(2)}, u32[]{:S(2)}) collective-permute-start(f32[8,1,66]{1,2,0:T(8,128)S(1)} %get-tuple-element.28), channel_id=1, source_target_pairs={{0,1},{1,2},{2,3},{4,5},{5,6},{6,7},{8,9},{9,10},{10,11},{12,13},{... | collective-permute-start | bytes 6344 | tf_op jit(solution)/shard_map/ppermute | solution.py:38
  143.6 4.5 %collective-permute-start.12 = (f32[8,32,1]{1,2,0:T(1,128)S(1)}, f32[8,32,1]{1,2,0:T(1,128)S(1)}, u32[]{:S(2)}, u32[]{:S(2)}) collective-permute-start(f32[8,32,1]{1,2,0:T(1,128)S(1)} %get-tuple-element.38), channel_id=1, source_target_pairs={{0,4},{4,8},{8,12},{12,16},{16,20},{20,24},{24,28},{1,5},{5,9},{9,... | collective-permute-start | bytes 3080 | tf_op jit(solution)/shard_map/ppermute | solution.py:38
  146.8 3.1 %collective-permute-start.13 = (f32[8,32,1]{1,2,0:T(1,128)S(1)}, f32[8,32,1]{1,2,0:T(1,128)S(1)}, u32[]{:S(2)}, u32[]{:S(2)}) collective-permute-start(f32[8,32,1]{1,2,0:T(1,128)S(1)} %get-tuple-element.39), channel_id=1, source_target_pairs={{4,0},{8,4},{12,8},{16,12},{20,16},{24,20},{28,24},{5,1},{9,5},{13... | collective-permute-start | bytes 3080 | tf_op jit(solution)/shard_map/ppermute | solution.py:39
  150.0 10.3 %collective-permute-start.14 = (f32[8,1,66]{1,2,0:T(8,128)S(1)}, f32[8,1,66]{1,2,0:T(8,128)S(1)}, u32[]{:S(2)}, u32[]{:S(2)}) collective-permute-start(f32[8,1,66]{1,2,0:T(8,128)S(1)} %get-tuple-element.27), channel_id=1, source_target_pairs={{1,0},{2,1},{3,2},{5,4},{6,5},{7,6},{9,8},{10,9},{11,10},{13,12},{... | collective-permute-start | bytes 6344 | tf_op jit(solution)/shard_map/ppermute | solution.py:39
  151.3 10.8 %collective-permute-start.15 = (f32[8,1,66]{1,2,0:T(8,128)S(1)}, f32[8,1,66]{1,2,0:T(8,128)S(1)}, u32[]{:S(2)}, u32[]{:S(2)}) collective-permute-start(f32[8,1,66]{1,2,0:T(8,128)S(1)} %get-tuple-element.26), channel_id=1, source_target_pairs={{0,1},{1,2},{2,3},{4,5},{5,6},{6,7},{8,9},{9,10},{10,11},{12,13},{... | collective-permute-start | bytes 6344 | tf_op jit(solution)/shard_map/ppermute | solution.py:38
  162.9 4.8 %collective-permute-start.16 = (f32[8,32,1]{1,2,0:T(1,128)S(1)}, f32[8,32,1]{1,2,0:T(1,128)S(1)}, u32[]{:S(2)}, u32[]{:S(2)}) collective-permute-start(f32[8,32,1]{1,2,0:T(1,128)S(1)} %get-tuple-element.36), channel_id=1, source_target_pairs={{0,4},{4,8},{8,12},{12,16},{16,20},{20,24},{24,28},{1,5},{5,9},{9,... | collective-permute-start | bytes 3080 | tf_op jit(solution)/shard_map/ppermute | solution.py:38
  166.4 3.1 %collective-permute-start.17 = (f32[8,32,1]{1,2,0:T(1,128)S(1)}, f32[8,32,1]{1,2,0:T(1,128)S(1)}, u32[]{:S(2)}, u32[]{:S(2)}) collective-permute-start(f32[8,32,1]{1,2,0:T(1,128)S(1)} %get-tuple-element.37), channel_id=1, source_target_pairs={{4,0},{8,4},{12,8},{16,12},{20,16},{24,20},{28,24},{5,1},{9,5},{13... | collective-permute-start | bytes 3080 | tf_op jit(solution)/shard_map/ppermute | solution.py:39
  169.6 10.4 %collective-permute-start.18 = (f32[8,1,66]{1,2,0:T(8,128)S(1)}, f32[8,1,66]{1,2,0:T(8,128)S(1)}, u32[]{:S(2)}, u32[]{:S(2)}) collective-permute-start(f32[8,1,66]{1,2,0:T(8,128)S(1)} %get-tuple-element.25), channel_id=1, source_target_pairs={{1,0},{2,1},{3,2},{5,4},{6,5},{7,6},{9,8},{10,9},{11,10},{13,12},{... | collective-permute-start | bytes 6344 | tf_op jit(solution)/shard_map/ppermute | solution.py:39
  170.9 10.9 %collective-permute-start.19 = (f32[8,1,66]{1,2,0:T(8,128)S(1)}, f32[8,1,66]{1,2,0:T(8,128)S(1)}, u32[]{:S(2)}, u32[]{:S(2)}) collective-permute-start(f32[8,1,66]{1,2,0:T(8,128)S(1)} %get-tuple-element.24), channel_id=1, source_target_pairs={{0,1},{1,2},{2,3},{4,5},{5,6},{6,7},{8,9},{9,10},{10,11},{12,13},{... | collective-permute-start | bytes 6344 | tf_op jit(solution)/shard_map/ppermute | solution.py:38
  182.6 4.8 %collective-permute-start.20 = (f32[8,32,1]{1,2,0:T(1,128)S(1)}, f32[8,32,1]{1,2,0:T(1,128)S(1)}, u32[]{:S(2)}, u32[]{:S(2)}) collective-permute-start(f32[8,32,1]{1,2,0:T(1,128)S(1)} %get-tuple-element.30), channel_id=1, source_target_pairs={{0,4},{4,8},{8,12},{12,16},{16,20},{20,24},{24,28},{1,5},{5,9},{9,... | collective-permute-start | bytes 3080 | tf_op jit(solution)/shard_map/ppermute | solution.py:38
  186.1 3.3 %collective-permute-start.21 = (f32[8,32,1]{1,2,0:T(1,128)S(1)}, f32[8,32,1]{1,2,0:T(1,128)S(1)}, u32[]{:S(2)}, u32[]{:S(2)}) collective-permute-start(f32[8,32,1]{1,2,0:T(1,128)S(1)} %get-tuple-element.31), channel_id=1, source_target_pairs={{4,0},{8,4},{12,8},{16,12},{20,16},{24,20},{28,24},{5,1},{9,5},{13... | collective-permute-start | bytes 3080 | tf_op jit(solution)/shard_map/ppermute | solution.py:39
  189.6 10.6 %collective-permute-start.22 = (f32[8,1,66]{1,2,0:T(8,128)S(1)}, f32[8,1,66]{1,2,0:T(8,128)S(1)}, u32[]{:S(2)}, u32[]{:S(2)}) collective-permute-start(f32[8,1,66]{1,2,0:T(8,128)S(1)} %get-tuple-element.23), channel_id=1, source_target_pairs={{1,0},{2,1},{3,2},{5,4},{6,5},{7,6},{9,8},{10,9},{11,10},{13,12},{... | collective-permute-start | bytes 6344 | tf_op jit(solution)/shard_map/ppermute | solution.py:39
  190.9 11.0 %collective-permute-start.23 = (f32[8,1,66]{1,2,0:T(8,128)S(1)}, f32[8,1,66]{1,2,0:T(8,128)S(1)}, u32[]{:S(2)}, u32[]{:S(2)}) collective-permute-start(f32[8,1,66]{1,2,0:T(8,128)S(1)} %get-tuple-element.22), channel_id=1, source_target_pairs={{0,1},{1,2},{2,3},{4,5},{5,6},{6,7},{8,9},{9,10},{10,11},{12,13},{... | collective-permute-start | bytes 6344 | tf_op jit(solution)/shard_map/ppermute | solution.py:38
  202.6 6.7 %collective-permute-start.24 = (f32[8,32,64]{1,2,0:T(8,128)S(1)}, f32[8,32,64]{1,2,0:T(8,128)S(1)}, u32[]{:S(2)}, u32[]{:S(2)}) collective-permute-start(f32[8,32,64]{1,2,0:T(8,128)S(1)} %fusion.4), channel_id=1, source_target_pairs={{0,4},{4,8},{8,12},{12,16},{16,20},{20,24},{24,28},{28,0},{1,5},{5... | collective-permute-start | bytes 196616 | tf_op jit(solution)/shard_map/ppermute | solution.py:21
  204.2 6.9 %collective-permute-start.25 = (f32[8,32,64]{1,2,0:T(8,128)S(1)}, f32[8,32,64]{1,2,0:T(8,128)S(1)}, u32[]{:S(2)}, u32[]{:S(2)}) collective-permute-start(f32[8,32,64]{1,2,0:T(8,128)S(1)} %fusion.4), channel_id=1, source_target_pairs={{0,28},{4,0},{8,4},{12,8},{16,12},{20,16},{24,20},{28,24},{1,29},{... | collective-permute-start | bytes 196616 | tf_op jit(solution)/shard_map/ppermute | solution.py:24
  209.4 6.8 %collective-permute-start.26 = (f32[8,32,64]{1,2,0:T(8,128)S(1)}, f32[8,32,64]{1,2,0:T(8,128)S(1)}, u32[]{:S(2)}, u32[]{:S(2)}) collective-permute-start(f32[8,32,64]{1,2,0:T(8,128)S(1)} %collective-permute-done.24), channel_id=1, source_target_pairs={{0,4},{4,8},{8,12},{12,16},{16,20},{20,24},{24,28},{28,0},{1,5},{5... | collective-permute-start | bytes 196616 | tf_op jit(solution)/shard_map/ppermute | solution.py:21
  211.1 7.7 %collective-permute-start.27 = (f32[8,32,64]{1,2,0:T(8,128)S(1)}, f32[8,32,64]{1,2,0:T(8,128)S(1)}, u32[]{:S(2)}, u32[]{:S(2)}) collective-permute-start(f32[8,32,64]{1,2,0:T(8,128)S(1)} %collective-permute-done.25), channel_id=1, source_target_pairs={{0,28},{4,0},{8,4},{12,8},{16,12},{20,16},{24,20},{28,24},{1,29},{... | collective-permute-start | bytes 196616 | tf_op jit(solution)/shard_map/ppermute | solution.py:24
  216.2 7.2 %collective-permute-start.28 = (f32[8,32,64]{1,2,0:T(8,128)S(1)}, f32[8,32,64]{1,2,0:T(8,128)S(1)}, u32[]{:S(2)}, u32[]{:S(2)}) collective-permute-start(f32[8,32,64]{1,2,0:T(8,128)S(1)} %collective-permute-done.26), channel_id=1, source_target_pairs={{0,4},{4,8},{8,12},{12,16},{16,20},{20,24},{24,28},{28,0},{1,5},{5... | collective-permute-start | bytes 196616 | tf_op jit(solution)/shard_map/ppermute | solution.py:21
  218.7 11.3 %collective-permute-start.29 = (f32[8,32,64]{1,2,0:T(8,128)S(1)}, f32[8,32,64]{1,2,0:T(8,128)}, u32[]{:S(2)}, u32[]{:S(2)}) collective-permute-start(f32[8,32,64]{1,2,0:T(8,128)S(1)} %collective-permute-done.27), channel_id=1, source_target_pairs={{0,28},{4,0},{8,4},{12,8},{16,12},{20,16},{24,20},{28,24},{1,29},{... | collective-permute-start | bytes 196616 | tf_op jit(solution)/shard_map/ppermute | solution.py:24
  223.4 9.3 %collective-permute-start.30 = (f32[8,32,64]{1,2,0:T(8,128)S(1)}, f32[8,32,64]{1,2,0:T(8,128)S(1)}, u32[]{:S(2)}, u32[]{:S(2)}) collective-permute-start(f32[8,32,64]{1,2,0:T(8,128)S(1)} %collective-permute-done.28), channel_id=1, source_target_pairs={{0,4},{4,8},{8,12},{12,16},{16,20},{20,24},{24,28},{28,0},{1,5},{5... | collective-permute-start | bytes 196616 | tf_op jit(solution)/shard_map/ppermute | solution.py:21
  228.3 6.1 %copy-start.9 = (bf16[32,32]{1,0:T(8,128)(2,1)S(1)}, bf16[32,32]{1,0:T(8,128)(2,1)}, u32[]{:S(2)}) copy-start(bf16[32,32]{1,0:T(8,128)(2,1)} %param.10) | copy-start | bytes 6148
  232.8 31.7 %copy-start.4 = (bf16[8,4,8,128]{3,2,1,0:T(8,128)(2,1)S(1)}, bf16[8,4,8,128]{3,2,1,0:T(8,128)(2,1)}, u32[]{:S(2)}) copy-start(bf16[8,4,8,128]{3,2,1,0:T(8,128)(2,1)} %param.8) | copy-start | bytes 196612
Sparse Core Ops, SparseCore 0:
  10.1 48.3 all-gather.1
  65.6 32.9 reduce-scatter.6
  235.8 28.6 reduce-scatter.4
